TPU v7x, 32 devices: a whole 2x2x4 slice. The times are simulated.
32 devices in a mesh: dp: 8 (over z, y), expert: 4 (over x, core).
Axes of the slice: x: 2, y: 2, z: 4, core: 2. Of those that a mesh axis runs over, the one named last changes fastest.
Arguments:
- tokens: bfloat16 [4096, 2048], P(('dp', 'expert')), may hold values from -6 to 6
- routes: int32 [4096, 8], P(('dp', 'expert')), may hold values from 0 to 15, all different within a row; in each aligned block of 128 rows (0 to 127, 128 to 255, ...) at most 80 rows name the same one
- gates: bfloat16 [4096, 8], P(('dp', 'expert')), may hold values from 0.099609375 to 0.5
- cotangent: bfloat16 [4096, 2048], P(('dp', 'expert')), may hold values from -6 to 6
- w_gate: bfloat16 [16, 2048, 384], P('dp'), may hold values from -0.125 to 0.125
- w_up: bfloat16 [16, 2048, 384], P('dp'), may hold values from -0.125 to 0.125
- w_down: bfloat16 [16, 384, 2048], P('dp'), may hold values from -0.3125 to 0.3125
Outputs:
- layer_out: bfloat16 [4096, 2048], P(('dp', 'expert'))
- grad_tokens: bfloat16 [4096, 2048], P(('dp', 'expert'))
- grad_gate: bfloat16 [16, 2048, 384], P('dp', 'expert')
- grad_up: bfloat16 [16, 2048, 384], P('dp', 'expert')
- grad_down: bfloat16 [16, 384, 2048], P('dp', None, 'expert')
Inputs may be any that keep to these rules, and one draw needn't show every extreme that they name: `routes`: each row names 8 different experts. Among the rows of one device, no expert is named by more than 80 rows, and in every draw some device has an expert named by exactly 80 rows.
All inputs are finite; a program needn't handle non-finite values.
Results may differ from a plain program's by a relative error of at most 0.012.
Values may be sent and summed in bfloat16 or wider, within the bound.
A program may use at most 128 MiB of HBM per device.

v0:
```python
import jax
import jax.numpy as jnp
from jax import lax
from jax.sharding import PartitionSpec as P


def expert_forward(arrived, w_gate, w_up, w_down):
    gate_act = jnp.einsum("erd,edf->erf", arrived, w_gate, preferred_element_type=jnp.float32)
    up_act = jnp.einsum("erd,edf->erf", arrived, w_up, preferred_element_type=jnp.float32)
    sigma_gate = jax.nn.sigmoid(gate_act)
    smooth = gate_act * sigma_gate
    hidden = (smooth * up_act).astype(jnp.bfloat16)
    result = jnp.einsum("erf,efd->erd", hidden, w_down, preferred_element_type=jnp.float32).astype(
        jnp.bfloat16
    )
    return (gate_act, up_act, sigma_gate, smooth, hidden, result)


def body(tokens, routes, gates, cotangent, w_gate, w_up, w_down):
    tok_rows, top_k = routes.shape
    width = tokens.shape[1]
    owners = lax.axis_size("dp")
    me = lax.axis_index("dp")
    per_owner = w_gate.shape[0]
    hidden_units = w_gate.shape[2]
    experts = owners * per_owner
    capacity = max(2, tok_rows * top_k * 5 // (4 * experts))
    rows_per_expert = owners * capacity
    both = jnp.concatenate([tokens, cotangent], axis=1)
    all_both = lax.all_gather(both, "dp", axis=0, tiled=True)
    all_routes = lax.all_gather(routes, "dp", axis=0, tiled=True)
    all_gates = lax.all_gather(gates, "dp", axis=0, tiled=True)
    all_x = all_both[:, :width]
    all_c = all_both[:, width:]
    mine = me * per_owner + jnp.arange(per_owner, dtype=jnp.int32)
    hit = all_routes[None, :, :] == mine[:, None, None]
    named = jnp.any(hit, axis=2).astype(jnp.int32)
    gain = jnp.sum(jnp.where(hit, all_gates[None, :, :].astype(jnp.float32), 0.0), axis=2)
    position = jnp.where(named > 0, jnp.cumsum(named, axis=1) - 1, -1)
    pick = position[:, None, :] == jnp.arange(rows_per_expert, dtype=jnp.int32)[None, :, None]
    pick_x = pick.astype(jnp.bfloat16)
    pick_g = jnp.where(pick, gain[:, None, :], 0.0).astype(jnp.bfloat16)
    arrived = jnp.einsum("ept,td->epd", pick_x, all_x, preferred_element_type=jnp.float32).astype(
        jnp.bfloat16
    )
    arrived_grad = jnp.einsum(
        "ept,td->epd", pick_g, all_c, preferred_element_type=jnp.float32
    ).astype(jnp.bfloat16)
    state = expert_forward(arrived, w_gate, w_up, w_down)
    gate_act, up_act, sigma_gate, smooth, hidden, result = state
    out_part = jnp.einsum("ept,epd->td", pick_g, result, preferred_element_type=jnp.float32).astype(
        jnp.bfloat16
    )
    layer_out = lax.psum_scatter(out_part, "dp", scatter_dimension=0, tiled=True)
    grad_hidden = jnp.einsum(
        "erd,efd->erf", arrived_grad, w_down, preferred_element_type=jnp.float32
    )
    grad_upact = (grad_hidden * smooth).astype(jnp.bfloat16)
    grad_gateact = (
        grad_hidden * up_act * sigma_gate * (1.0 + gate_act * (1.0 - sigma_gate))
    ).astype(jnp.bfloat16)
    row_grads = (
        jnp.einsum("erf,edf->erd", grad_gateact, w_gate, preferred_element_type=jnp.float32)
        + jnp.einsum("erf,edf->erd", grad_upact, w_up, preferred_element_type=jnp.float32)
    ).astype(jnp.bfloat16)
    grad_part = jnp.einsum(
        "ept,epd->td", pick_x, row_grads, preferred_element_type=jnp.float32
    ).astype(jnp.bfloat16)
    grad_tokens = lax.psum_scatter(grad_part, "dp", scatter_dimension=0, tiled=True)
    both_factors = jnp.concatenate([grad_gateact, grad_upact], axis=2)
    input_term = jnp.einsum(
        "erd,erf->def", arrived, both_factors, preferred_element_type=jnp.float32
    )
    down_term = jnp.einsum("erf,erd->def", hidden, arrived_grad, preferred_element_type=jnp.float32)
    totals = lax.psum_scatter(
        jnp.concatenate([input_term, down_term], axis=2).astype(jnp.bfloat16),
        "expert",
        scatter_dimension=0,
        tiled=True,
    ).astype(jnp.float32)
    grad_gate = jnp.transpose(totals[:, :, :hidden_units], (1, 0, 2)).astype(jnp.bfloat16)
    grad_up = jnp.transpose(totals[:, :, hidden_units : 2 * hidden_units], (1, 0, 2)).astype(
        jnp.bfloat16
    )
    grad_down = jnp.transpose(totals[:, :, 2 * hidden_units :], (1, 2, 0)).astype(jnp.bfloat16)
    return (layer_out, grad_tokens, grad_gate, grad_up, grad_down)


def solution(mesh):
    return jax.shard_map(
        body,
        mesh=mesh,
        in_specs=(
            P(("dp", "expert"), None),
            P(("dp", "expert"), None),
            P(("dp", "expert"), None),
            P(("dp", "expert"), None),
            P("dp", None, None),
            P("dp", None, None),
            P("dp", None, None),
        ),
        out_specs=(
            P(("dp", "expert"), None),
            P(("dp", "expert"), None),
            P("dp", "expert", None),
            P("dp", "expert", None),
            P("dp", None, "expert"),
        ),
        check_vma=False,
    )
```

profile of v0, /device:TPU:0, one launch (start us, length us, event | category | flops | bytes accessed | tf_op | source)
XLA Modules:
  0.0 451.6 jit_solution(4144293296469988950)
XLA Ops:
  7.2 0.0 copy-start
  7.2 0.0 all-gather.2.cloned.1.call-start
  7.2 2.5 pad_maximum_fusion.1
  9.7 0.0 all-gather.2.cloned.1.call-update
  9.7 0.0 reduce-scatter.8.cloned.1.call-start
  9.8 28.8 %all_gather.10 = bf16[1024,8]{0,1:T(8,128)(2,1)S(1)} all-gather(bf16[128,8]{0,1:T(8,128)(2,1)} %param.9), channel_id=1, replica_groups=mesh['dp'=8,'expert'=4] {'dp'}, dimensions={0}, use_global_device_ids=true | all-gather | bytes 18432 | tf_op jit(solution)/shard_map/all_gather | solution.py:32
  38.6 31.7 %all_gather.9 = s32[1024,8]{0,1:T(8,128)S(1)} all-gather(s32[128,8]{0,1:T(8,128)} %param.8), channel_id=1, replica_groups=mesh['dp'=8,'expert'=4] {'dp'}, dimensions={0}, use_global_device_ids=true | all-gather | bytes 36864 | tf_op jit(solution)/shard_map/all_gather | solution.py:31
  70.3 0.1 compare_reduce_fusion
  70.4 0.6 reduce-window.6
  71.0 0.2 slice_reduce_fusion
  71.2 0.2 reduce-window.9
  71.4 0.1 fusion.26
  71.5 0.1 add_bitcast_fusion
  71.6 66.1 %all-gather.2.cloned.1.call-done = bf16[1024,4096]{1,0:T(8,128)(2,1)} async-done(((bf16[128,4096]{1,0:T(8,128)(2,1)}), bf16[1024,4096]{1,0:T(8,128)(2,1)}) %all-gather.2.cloned.1.call-update) | async-done | bytes 8388624 | tf_op jit(solution)/shard_map/all_gather | solution.py:30
  137.7 8.4 %fusion.6 = bf16[2,640,2048]{2,1,0:T(8,128)(2,1)S(1)} fusion(bf16[1024,4096]{1,0:T(8,128)(2,1)} %all-gather.2.cloned.1.call-done, s32[2,1024]{1,0:T(2,128)S(1)} %compare_select_fusion.1), kind=kOutput, calls=%fused_computation.15 | convolution fusion | flops 5372641280 | bytes 9445376 | tf_op jit(solution)/shard_map/ept,td->epd/dot_general | solution.py:43
  146.1 0.0 copy-done.3
  146.1 0.0 copy-start.1
  146.1 0.0 slice-start
  146.2 2.9 fusion.31
  149.0 0.0 copy-done.1
  149.1 0.0 slice-start.1
  149.1 4.1 fusion.30
  153.2 0.0 slice-done
  153.2 0.0 slice-done.1
  153.2 7.9 %fusion.5 = bf16[2,640,2048]{2,1,0:T(8,128)(2,1)} fusion(bf16[1024,4096]{1,0:T(8,128)(2,1)S(1)} %bitcast.63, bf16[2,1024]{1,0:T(2,128)(2,1)S(1)} %fusion.26, s32[2,1024]{1,0:T(2,128)S(1)} %compare_select_fusion.1), kind=kOutput, calls=%fused_computation.14 | convolution fusion | flops 5373952000 | bytes 9449472 | tf_op jit(solution)/shard_map/ept,td->epd/dot_general | solution.py:46
  161.1 0.0 copy-done
  161.1 6.5 %multiply_convert_fusion = (bf16[2,640,384]{1,2,0:T(8,128)(2,1)S(1)}, bf16[2,640,384]{1,2,0:T(8,128)(2,1)S(1)}, bf16[2,640,384]{1,2,0:T(8,128)(2,1)S(1)}) fusion(f32[2,640,384]{1,2,0:T(8,128)} %fusion.30, f32[2,640,384]{1,2,0:T(8,128)S(1)} %fusion.31, bf16[2,640,2048]{2,1,0:T(8,128)(2,1)} %fusion.5, bf16[2,384,2048]{2,1,0:T(8,128)(2,1)S(1)} %copy-done), kind=kOutput, calls=%fused_computation.30 | convolution fusion | flops 2020638720 | bytes 15269888 | tf_op jit(solution)/shard_map/erd,efd->erf/dot_general | solution.py:55
  167.7 2.9 fusion.9
  170.5 0.0 copy-done.4
  170.5 0.0 copy-done.2
  170.6 0.0 copy-done.6
  170.6 5.3 %convert_bitcast_fusion = bf16[2048,2,768]{0,2,1:T(8,128)(2,1)S(1)} fusion(bf16[2,640,2048]{2,1,0:T(8,128)(2,1)S(1)} %fusion.6, bf16[2,640,384]{1,2,0:T(8,128)(2,1)S(1)} %get-tuple-element.20, bf16[2,640,384]{1,2,0:T(8,128)(2,1)S(1)} %get-tuple-element.21), kind=kOutput, calls=%fused_computation.4 | convolution fusion | flops 4033609728 | bytes 13500416 | tf_op jit(solution)/shard_map/erd,erf->def/dot_general | solution.py:71
  175.9 8.5 %pad_maximum_fusion = bf16[2048,2,1152]{0,2,1:T(8,128)(2,1)} fusion(bf16[2048,2,384]{0,2,1:T(8,128)(2,1)S(1)} %fusion.9, bf16[2048,2,768]{0,2,1:T(8,128)(2,1)S(1)} %convert_bitcast_fusion), kind=kLoop, calls=%fused_computation.1 | loop fusion | flops 18874368 | bytes 18874368 | tf_op jit(solution)/shard_map/concatenate | solution.py:76
  184.3 0.0 reduce-scatter.8.cloned.1.call-update
  184.4 0.0 reduce-scatter.4.cloned.1.call-start
  184.4 4.4 fusion.59
  188.8 7.4 %bitcast_convert_fusion.1 = bf16[1024,2048]{1,0:T(8,128)(2,1)} fusion(bf16[2,1024]{1,0:T(2,128)(2,1)S(1)} %fusion.26, s32[2,1024]{1,0:T(2,128)S(1)} %compare_select_fusion.1, bf16[2,640,2048]{2,1,0:T(8,128)(2,1)S(1)} %fusion.59), kind=kOutput, calls=%fused_computation.3 | convolution fusion | flops 5373427712 | bytes 9449472 | tf_op jit(solution)/shard_map/ept,epd->td/dot_general | solution.py:51
  196.2 0.0 reduce-scatter.4.cloned.1.call-update
  196.2 0.3 reduce-scatter.6.cloned.1.call-start
  196.5 9.6 %fusion.32 = f32[2,640,2048]{2,1,0:T(8,128)} fusion(bf16[2,640,384]{1,2,0:T(8,128)(2,1)} %copy-done.2, bf16[2,2048,384]{2,1,0:T(8,128)(2,1)} %param.11), kind=kOutput, calls=%fused_computation.54 | convolution fusion | flops 2013265920 | bytes 14614528 | tf_op jit(solution)/shard_map/erf,edf->erd/dot_general | solution.py:63
  206.1 16.5 %bitcast_convert_fusion = bf16[1024,2048]{1,0:T(8,128)(2,1)} fusion(f32[2,640,2048]{2,1,0:T(8,128)} %fusion.32, s32[2,1024]{1,0:T(2,128)S(1)} %compare_select_fusion.1, bf16[2,640,384]{1,2,0:T(8,128)(2,1)} %copy-done.6, bf16[2,2048,384]{2,1,0:T(8,128)(2,1)} %param.12), kind=kOutput, calls=%fused_computation.2 | convolution fusion | flops 7390625792 | bytes 18817024 | tf_op jit(solution)/shard_map/ept,epd->td/dot_general | solution.py:66
  222.6 0.0 reduce-scatter.6.cloned.1.call-update
  222.6 37.9 %reduce-scatter.8.cloned.1.call-done = bf16[512,2,1152]{0,2,1:T(8,128)(2,1)} async-done(((bf16[2048,2,1152]{0,2,1:T(8,128)(2,1)}), bf16[512,2,1152]{0,2,1:T(8,128)(2,1)}) %reduce-scatter.8.cloned.1.call-update) | async-done | bytes 2359312 | tf_op jit(solution)/shard_map/reduce_scatter | solution.py:75
  260.5 3.1 slice_bitcast_fusion.8
  263.6 2.3 copy.36
  265.8 2.3 copy.35
  268.1 84.9 %reduce-scatter.4.cloned.1.call-done = bf16[128,2048]{1,0:T(8,128)(2,1)} async-done(((bf16[1024,2048]{1,0:T(8,128)(2,1)}), bf16[128,2048]{1,0:T(8,128)(2,1)}) %reduce-scatter.4.cloned.1.call-update) | async-done | bytes 524304 | tf_op jit(solution)/shard_map/reduce_scatter | solution.py:54
  353.1 92.0 %reduce-scatter.6.cloned.1.call-done = bf16[128,2048]{1,0:T(8,128)(2,1)} async-done(((bf16[1024,2048]{1,0:T(8,128)(2,1)}), bf16[128,2048]{1,0:T(8,128)(2,1)}) %reduce-scatter.6.cloned.1.call-update) | async-done | bytes 524304 | tf_op jit(solution)/shard_map/reduce_scatter | solution.py:69
  (12 shorter events, 0.0 us)
Async XLA Ops:
  7.2 154.0 %copy-start = (bf16[2,384,2048]{2,1,0:T(8,128)(2,1)S(1)}, bf16[2,384,2048]{2,1,0:T(8,128)(2,1)}, u32[]{:S(2)}) copy-start(bf16[2,384,2048]{2,1,0:T(8,128)(2,1)} %param.13) | copy-start | bytes 9437188
  7.2 130.6 %all-gather.2.cloned.1.call-start = ((), (), s32[]{:S(2)}) async-start(), calls=%async_computation.3 | async-start | bytes 9437184 | tf_op jit(solution)/shard_map/all_gather | solution.py:30
  9.7 250.8 %reduce-scatter.8.cloned.1.call-start = ((), (), s32[]{:S(2)}) async-start(), calls=%async_computation.6 | async-start | bytes 11796480 | tf_op jit(solution)/shard_map/reduce_scatter | solution.py:75
  137.7 8.4 %copy-start.3 = (bf16[2,2048,384]{2,1,0:T(8,128)(2,1)S(1)}, bf16[2,2048,384]{2,1,0:T(8,128)(2,1)}, u32[]{:S(2)}) copy-start(bf16[2,2048,384]{2,1,0:T(8,128)(2,1)} %param.12) | copy-start | bytes 9437188
  146.1 2.9 copy-start.1
  146.1 7.1 %slice-start = ((s8[8388608]{0:T(1024)(128)(4,1)}), s8[4194304]{0:T(1024)(128)(4,1)S(1)}, s32[]{:S(2)}) async-start(s8[8388608]{0:T(1024)(128)(4,1)} %bitcast.62), calls=%async_computation.7 | async-start | bytes 8388608
  149.1 4.2 slice-start.1
  161.1 6.5 %copy-start.5 = (bf16[2,640,2048]{2,1,0:T(8,128)(2,1)S(1)}, bf16[2,640,2048]{2,1,0:T(8,128)(2,1)}, u32[]{:S(2)}) copy-start(bf16[2,640,2048]{2,1,0:T(8,128)(2,1)} %fusion.5) | copy-start | bytes 15728644
  167.6 2.9 copy-start.4
  167.6 2.9 copy-start.2
  167.6 2.9 copy-start.6
  184.4 168.7 %reduce-scatter.4.cloned.1.call-start = ((), (), s32[]{:S(2)}) async-start(), calls=%async_computation.4 | async-start | bytes 4718592 | tf_op jit(solution)/shard_map/reduce_scatter | solution.py:54
  196.2 248.8 %reduce-scatter.6.cloned.1.call-start = ((), (), s32[]{:S(2)}) async-start(), calls=%async_computation.5 | async-start | bytes 4718592 | tf_op jit(solution)/shard_map/reduce_scatter | solution.py:69
Sparse Core Ops, SparseCore 0:
  10.1 127.5 all-gather.1
  184.5 75.9 reduce-scatter.7
  264.7 88.2 reduce-scatter.3
  357.1 87.9 reduce-scatter.5
where the time goes:
time: 452 us
  waiting for transfers between devices  281 us (62%)
  matrix products  75.8 us (17%)
  blocking collectives  60.5 us (13%)
  between operations  14 us (3%)
  other arithmetic  12 us (3%)
  local copies, waits for them, and re-layouts  7.89 us (2%)
    reduce_scatter x1, waiting for transfers between devices, body(): lax.psum_scatter(grad_part, 'dp', scatter_dimension=0, tiled=True)  92 us
    reduce_scatter x1, waiting for transfers between devices, body(): lax.psum_scatter(out_part, 'dp', scatter_dimension=0, tiled=True)  84.9 us
    all_gather x1, waiting for transfers between devices, body(): all_both = lax.all_gather(both, 'dp', axis=0, tiled=True)  66.1 us
    reduce_scatter x1, waiting for transfers between devices, body(): lax.psum_scatter(jnp.concatenate([input_term, down_term], axis=2).astype(...  37.9 us
    all_gather x1, blocking collectives, body(): all_routes = lax.all_gather(routes, 'dp', axis=0, tiled=True)  31.7 us
    all_gather x1, blocking collectives, body(): all_gates = lax.all_gather(gates, 'dp', axis=0, tiled=True)  28.8 us
    dot_general x1, matrix products, body(): jnp.einsum('ept,epd->td', pick_x, row_grads, preferred_element_type=jnp.f...  16.5 us
    dot_general x1, matrix products, body(): jnp.einsum('erf,edf->erd', grad_gateact, w_gate, preferred_element_type=j...  9.57 us
  transfers between devices with their start and end apart: 4, of which 4 were waited for; matrix products, arithmetic and copies ran while one was open for 10% of the time, Pallas kernels for 0%

commit v1 on v0

--- a/solution.py
+++ b/solution.py
@@ -2,6 +2,24 @@
 import jax.numpy as jnp
 from jax import lax
 from jax.sharding import PartitionSpec as P
+
+
+def joined_along(blocks, dim):
+    blocks = jnp.moveaxis(blocks, 0, dim)
+    shape = blocks.shape
+    return blocks.reshape(*shape[:dim], shape[dim] * shape[dim + 1], *shape[dim + 2 :])
+
+
+def grow_blocks(x, axis):
+    peers = lax.axis_size(axis)
+    parts = x[None]
+    for level in range(peers.bit_length() - 1):
+        bit = 1 << level
+        partner_block = lax.ppermute(parts, axis, [(i, i ^ bit) for i in range(peers)])
+        both = jnp.stack([parts, partner_block])
+        upper = lax.axis_index(axis) >> level & 1
+        parts = jnp.where(upper == 0, both, both[::-1]).reshape(-1, *x.shape)
+    return parts
 
 
 def expert_forward(arrived, w_gate, w_up, w_down):
@@ -27,7 +45,7 @@
     capacity = max(2, tok_rows * top_k * 5 // (4 * experts))
     rows_per_expert = owners * capacity
     both = jnp.concatenate([tokens, cotangent], axis=1)
-    all_both = lax.all_gather(both, "dp", axis=0, tiled=True)
+    all_both = joined_along(grow_blocks(both, "dp"), 0)
     all_routes = lax.all_gather(routes, "dp", axis=0, tiled=True)
     all_gates = lax.all_gather(gates, "dp", axis=0, tiled=True)
     all_x = all_both[:, :width]

time: 452 us -> 674 us (1.49)
  blocking collectives: 60.5 us -> 231 us
  other arithmetic: 12 us -> 40.3 us
  matrix products: 75.8 us -> 83.7 us
  starting transfers between devices: 0.38 us -> 7.63 us
    all_gather x1, blocking collectives: 28.8 us -> 200 us  [body(): all_gates = lax.all_gather(gates, 'dp', axis=0, tiled=True)]
    ppermute x0 -> x3, waiting for transfers between devices: none -> 68.8 us  [grow_blocks(): lax.ppermute(parts, axis, [(i, i ^ bit) for i in range(peers)])]
    all_gather x1 -> x0, waiting for transfers between devices: 66.1 us -> none  [body(): all_both = lax.all_gather(both, 'dp', axis=0, tiled=True)]
    select_n x0 -> x2, other arithmetic: none -> 16.4 us  [grow_blocks(): parts = jnp.where(upper == 0, both, both[::-1]).reshape(-1, *x.shape)]
    another operation x2 -> x6, other arithmetic: 0.77 us -> 15.1 us  [the longest x4 14.3 us: grow_blocks(): both = jnp.stack([parts, partner_block])]
    dot_general x1, matrix products: 7.89 us -> 17.6 us  [body(): jnp.einsum('ept,td->epd', pick_g, all_c, preferred_element_type=jnp.float32)]
    ppermute x0 -> x3, starting transfers between devices: none -> 7.33 us  [grow_blocks(): lax.ppermute(parts, axis, [(i, i ^ bit) for i in range(peers)])]
  transfers between devices with their start and end apart: 4 -> 6, of which waited for: 4 -> 5; matrix products, arithmetic and copies ran while one was open for 10% -> 7% of each run, Pallas kernels for 0% -> 0%
where the time goes in v1:
time: 674 us; the launch traced here: 671 us
  waiting for transfers between devices  283 us (42%)
  blocking collectives  231 us (34%)
  matrix products  83.7 us (12%)
  other arithmetic  40.3 us (6%)
  between operations  14.2 us (2%)
  local copies, waits for them, and re-layouts  11.9 us (2%)
  starting transfers between devices  7.63 us (1%)
    all_gather x1, blocking collectives, body(): all_gates = lax.all_gather(gates, 'dp', axis=0, tiled=True)  200 us
    reduce_scatter x1, waiting for transfers between devices, body(): lax.psum_scatter(grad_part, 'dp', scatter_dimension=0, tiled=True)  92.2 us
    reduce_scatter x1, waiting for transfers between devices, body(): lax.psum_scatter(out_part, 'dp', scatter_dimension=0, tiled=True)  84.9 us
    ppermute x3, waiting for transfers between devices, grow_blocks(): lax.ppermute(parts, axis, [(i, i ^ bit) for i in range(peers)])  68.8 us
    reduce_scatter x1, waiting for transfers between devices, body(): lax.psum_scatter(jnp.concatenate([input_term, down_term], axis=2).astype(...  37.2 us
    all_gather x1, blocking collectives, body(): all_routes = lax.all_gather(routes, 'dp', axis=0, tiled=True)  31 us
    dot_general x1, matrix products, body(): jnp.einsum('ept,td->epd', pick_g, all_c, preferred_element_type=jnp.float32)  17.6 us
    select_n x2, other arithmetic, grow_blocks(): parts = jnp.where(upper == 0, both, both[::-1]).reshape(-1, *x.shape)  16.4 us
  transfers between devices with their start and end apart: 6, of which 5 were waited for; matrix products, arithmetic and copies ran while one was open for 7% of the time, Pallas kernels for 0%

profile of v1, /device:TPU:0, one launch (start us, length us, event | category | flops | bytes accessed | tf_op | source)
XLA Modules:
  0.0 671.5 jit_solution(12233276144147664108)
XLA Ops:
  7.2 0.0 copy-start
  7.2 0.0 reduce-scatter.8.cloned.1.call-start
  7.2 2.1 constant_dynamic-update-slice_fusion.1
  9.3 1.9 constant_dynamic-update-slice_fusion
  11.2 3.0 collective-permute-start
  14.2 23.5 %collective-permute-done = bf16[1,128,4096]{2,1,0:T(8,128)(2,1)} collective-permute-done((bf16[1,128,4096]{2,1,0:T(8,128)(2,1)}, bf16[1,128,4096]{2,1,0:T(8,128)(2,1)}, u32[]{:S(2)}, u32[]{:S(2)}) %collective-permute-start) | collective-permute-done | bytes 1048608 | tf_op jit(solution)/shard_map/ppermute | solution.py:18
  37.7 1.7 pad_maximum_fusion.3
  39.4 2.6 fusion.25
  42.0 1.8 collective-permute-start.1
  43.8 45.3 %collective-permute-done.1 = bf16[2,128,4096]{2,1,0:T(8,128)(2,1)} collective-permute-done((bf16[2,128,4096]{2,1,0:T(8,128)(2,1)}, bf16[2,128,4096]{2,1,0:T(8,128)(2,1)}, u32[]{:S(2)}, u32[]{:S(2)}) %collective-permute-start.1) | collective-permute-done | bytes 2097184 | tf_op jit(solution)/shard_map/ppermute | solution.py:18
  89.1 2.6 pad_maximum_fusion.2
  91.7 0.0 copy-start.5
  91.7 2.9 reverse_select_fusion.1
  94.6 2.5 collective-permute-start.2
  97.1 199.7 %all_gather.7 = bf16[1024,8]{0,1:T(8,128)(2,1)S(1)} all-gather(bf16[128,8]{0,1:T(8,128)(2,1)S(1)} %copy-done.5), channel_id=1, replica_groups=mesh['dp'=8,'expert'=4] {'dp'}, dimensions={0}, use_global_device_ids=true | all-gather | bytes 18432 | tf_op jit(solution)/shard_map/all_gather | solution.py:50
  296.9 31.0 %all_gather.6 = s32[1024,8]{0,1:T(8,128)S(1)} all-gather(s32[128,8]{0,1:T(8,128)S(1)} %copy-done.4), channel_id=1, replica_groups=mesh['dp'=8,'expert'=4] {'dp'}, dimensions={0}, use_global_device_ids=true | all-gather | bytes 36864 | tf_op jit(solution)/shard_map/all_gather | solution.py:49
  327.9 0.1 compare_reduce_fusion
  328.0 0.6 reduce-window.6
  328.6 0.2 slice_reduce_fusion
  328.8 0.2 reduce-window.9
  329.0 0.1 fusion.28
  329.1 0.1 add_bitcast_fusion
  329.2 7.5 %pad_maximum_fusion.1 = bf16[2,4,128,4096]{3,2,1,0:T(8,128)(2,1)} fusion(bf16[1,4,128,4096]{3,2,1,0:T(8,128)(2,1)} %bitcast.8, bf16[1,4,128,4096]{3,2,1,0:T(8,128)(2,1)} %bitcast.6), kind=kLoop, calls=%fused_computation.3 | loop fusion | flops 4194304 | bytes 16777216 | tf_op jit(solution)/shard_map/stack | solution.py:19
  336.6 13.5 %reverse_select_fusion = bf16[2,4,128,4096]{3,2,1,0:T(8,128)(2,1)} fusion(bf16[2,4,128,4096]{3,2,1,0:T(8,128)(2,1)} %pad_maximum_fusion.1, pred[]{:T(512)S(6)} %eq.41), kind=kLoop, calls=%fused_computation | loop fusion | flops 4194304 | bytes 16777216 | tf_op jit(solution)/shard_map/jit(_where)/select_n | solution.py:21
  350.2 8.4 %fusion.6 = bf16[2,640,2048]{2,1,0:T(8,128)(2,1)S(1)} fusion(bf16[1024,4096]{1,0:T(8,128)(2,1)} %bitcast.72, s32[2,1024]{1,0:T(2,128)S(1)} %compare_select_fusion.1), kind=kOutput, calls=%fused_computation.19 | convolution fusion | flops 5372641280 | bytes 9445376 | tf_op jit(solution)/shard_map/ept,td->epd/dot_general | solution.py:61
  358.6 0.0 copy-start.6
  358.6 17.6 %fusion.5 = bf16[2,640,2048]{2,1,0:T(8,128)(2,1)S(1)} fusion(bf16[1024,4096]{1,0:T(8,128)(2,1)S(1)} %bitcast.73, bf16[2,1024]{1,0:T(2,128)(2,1)S(1)} %fusion.28, s32[2,1024]{1,0:T(2,128)S(1)} %compare_select_fusion.1), kind=kOutput, calls=%fused_computation.18 | convolution fusion | flops 5373952000 | bytes 9449472 | tf_op jit(solution)/shard_map/ept,td->epd/dot_general | solution.py:64
  376.2 2.9 fusion.33
  379.1 4.1 fusion.32
  383.2 4.9 multiply_convert_fusion
  388.2 2.9 fusion.9
  391.1 5.3 convert_bitcast_fusion
  396.4 8.5 %pad_maximum_fusion = bf16[2048,2,1152]{0,2,1:T(8,128)(2,1)} fusion(bf16[2048,2,384]{0,2,1:T(8,128)(2,1)S(1)} %fusion.9, bf16[2048,2,768]{0,2,1:T(8,128)(2,1)S(1)} %convert_bitcast_fusion), kind=kLoop, calls=%fused_computation.2 | loop fusion | flops 18874368 | bytes 18874368 | tf_op jit(solution)/shard_map/concatenate | solution.py:94
  404.8 0.0 reduce-scatter.8.cloned.1.call-update
  404.9 0.0 reduce-scatter.4.cloned.1.call-start
  404.9 4.4 fusion.61
  409.3 7.4 %bitcast_convert_fusion.1 = bf16[1024,2048]{1,0:T(8,128)(2,1)} fusion(bf16[2,1024]{1,0:T(2,128)(2,1)S(1)} %fusion.28, s32[2,1024]{1,0:T(2,128)S(1)} %compare_select_fusion.1, bf16[2,640,2048]{2,1,0:T(8,128)(2,1)S(1)} %fusion.61), kind=kOutput, calls=%fused_computation.5 | convolution fusion | flops 5373427712 | bytes 9449472 | tf_op jit(solution)/shard_map/ept,epd->td/dot_general | solution.py:69
  416.7 0.0 reduce-scatter.4.cloned.1.call-update
  416.7 0.2 reduce-scatter.6.cloned.1.call-start
  416.9 9.8 %fusion.34 = f32[2,640,2048]{2,1,0:T(8,128)} fusion(bf16[2,640,384]{1,2,0:T(8,128)(2,1)} %copy-done.3, bf16[2,2048,384]{2,1,0:T(8,128)(2,1)} %param.11), kind=kOutput, calls=%fused_computation.63 | convolution fusion | flops 2013265920 | bytes 14614528 | tf_op jit(solution)/shard_map/erf,edf->erd/dot_general | solution.py:81
  426.7 16.1 %bitcast_convert_fusion = bf16[1024,2048]{1,0:T(8,128)(2,1)} fusion(f32[2,640,2048]{2,1,0:T(8,128)} %fusion.34, s32[2,1024]{1,0:T(2,128)S(1)} %compare_select_fusion.1, bf16[2,640,384]{1,2,0:T(8,128)(2,1)} %copy-done.8, bf16[2,2048,384]{2,1,0:T(8,128)(2,1)} %param.12), kind=kOutput, calls=%fused_computation.4 | convolution fusion | flops 7390625792 | bytes 18817024 | tf_op jit(solution)/shard_map/ept,epd->td/dot_general | solution.py:84
  442.8 0.0 reduce-scatter.6.cloned.1.call-update
  442.8 37.2 %reduce-scatter.8.cloned.1.call-done = bf16[512,2,1152]{0,2,1:T(8,128)(2,1)} async-done(((bf16[2048,2,1152]{0,2,1:T(8,128)(2,1)}), bf16[512,2,1152]{0,2,1:T(8,128)(2,1)}) %reduce-scatter.8.cloned.1.call-update) | async-done | bytes 2359312 | tf_op jit(solution)/shard_map/reduce_scatter | solution.py:93
  480.0 3.1 slice_bitcast_fusion.8
  483.1 2.3 copy.36
  485.4 2.3 copy.35
  487.7 84.9 %reduce-scatter.4.cloned.1.call-done = bf16[128,2048]{1,0:T(8,128)(2,1)} async-done(((bf16[1024,2048]{1,0:T(8,128)(2,1)}), bf16[128,2048]{1,0:T(8,128)(2,1)}) %reduce-scatter.4.cloned.1.call-update) | async-done | bytes 524304 | tf_op jit(solution)/shard_map/reduce_scatter | solution.py:72
  572.6 92.2 %reduce-scatter.6.cloned.1.call-done = bf16[128,2048]{1,0:T(8,128)(2,1)} async-done(((bf16[1024,2048]{1,0:T(8,128)(2,1)}), bf16[128,2048]{1,0:T(8,128)(2,1)}) %reduce-scatter.6.cloned.1.call-update) | async-done | bytes 524304 | tf_op jit(solution)/shard_map/reduce_scatter | solution.py:87
  (21 shorter events, 0.1 us)
Async XLA Ops:
  7.2 376.0 %copy-start = (bf16[2,384,2048]{2,1,0:T(8,128)(2,1)S(1)}, bf16[2,384,2048]{2,1,0:T(8,128)(2,1)}, u32[]{:S(2)}) copy-start(bf16[2,384,2048]{2,1,0:T(8,128)(2,1)} %param.13) | copy-start | bytes 9437188
  7.2 472.8 %reduce-scatter.8.cloned.1.call-start = ((), (), s32[]{:S(2)}) async-start(), calls=%async_computation.5 | async-start | bytes 11796480 | tf_op jit(solution)/shard_map/reduce_scatter | solution.py:93
  11.2 26.5 %collective-permute-start = (bf16[1,128,4096]{2,1,0:T(8,128)(2,1)}, bf16[1,128,4096]{2,1,0:T(8,128)(2,1)}, u32[]{:S(2)}, u32[]{:S(2)}) collective-permute-start(bf16[1,128,4096]{2,1,0:T(8,128)(2,1)} %bitcast.1), channel_id=1, source_target_pairs={{0,4},{4,0},{8,12},{12,8},{16,20},{20,16},{24,28},{28,24},{1,5},{5... | collective-permute-start | bytes 3145736 | tf_op jit(solution)/shard_map/ppermute | solution.py:18
  42.0 47.1 %collective-permute-start.1 = (bf16[2,128,4096]{2,1,0:T(8,128)(2,1)}, bf16[2,128,4096]{2,1,0:T(8,128)(2,1)}, u32[]{:S(2)}, u32[]{:S(2)}) collective-permute-start(bf16[2,128,4096]{2,1,0:T(8,128)(2,1)} %get-tuple-element.27), channel_id=1, source_target_pairs={{0,8},{4,12},{8,0},{12,4},{16,24},{20,28},{24,16},{28,20},{1,9},{5... | collective-permute-start | bytes 6291464 | tf_op jit(solution)/shard_map/ppermute | solution.py:18
  91.7 5.5 copy-start.5
  91.7 205.2 %copy-start.4 = (s32[128,8]{0,1:T(8,128)S(1)}, s32[128,8]{0,1:T(8,128)}, u32[]{:S(2)}) copy-start(s32[128,8]{0,1:T(8,128)} %param.8) | copy-start | bytes 12292
  94.6 234.6 %collective-permute-start.2 = (bf16[4,128,4096]{2,1,0:T(8,128)(2,1)}, bf16[4,128,4096]{2,1,0:T(8,128)(2,1)}, u32[]{:S(2)}, u32[]{:S(2)}) collective-permute-start(bf16[4,128,4096]{2,1,0:T(8,128)(2,1)} %bitcast.7), channel_id=1, source_target_pairs={{0,16},{4,20},{8,24},{12,28},{16,0},{20,4},{24,8},{28,12},{1,17},{... | collective-permute-start | bytes 12582920 | tf_op jit(solution)/shard_map/ppermute | solution.py:18
  350.2 8.4 %copy-start.1 = (bf16[2,4,128,4096]{3,2,1,0:T(8,128)(2,1)S(1)}, bf16[2,4,128,4096]{3,2,1,0:T(8,128)(2,1)}, u32[]{:S(2)}) copy-start(bf16[2,4,128,4096]{3,2,1,0:T(8,128)(2,1)} %reverse_select_fusion) | copy-start | bytes 25165828
  358.6 17.6 %copy-start.6 = (bf16[2,2048,384]{2,1,0:T(8,128)(2,1)S(1)}, bf16[2,2048,384]{2,1,0:T(8,128)(2,1)}, u32[]{:S(2)}) copy-start(bf16[2,2048,384]{2,1,0:T(8,128)(2,1)} %param.12) | copy-start | bytes 9437188
  376.2 2.9 copy-start.2
  388.1 2.9 copy-start.7
  388.1 2.9 copy-start.3
  388.2 2.9 copy-start.8
  404.9 167.7 %reduce-scatter.4.cloned.1.call-start = ((), (), s32[]{:S(2)}) async-start(), calls=%async_computation.3 | async-start | bytes 4718592 | tf_op jit(solution)/shard_map/reduce_scatter | solution.py:72
  416.7 248.0 %reduce-scatter.6.cloned.1.call-start = ((), (), s32[]{:S(2)}) async-start(), calls=%async_computation.4 | async-start | bytes 4718592 | tf_op jit(solution)/shard_map/reduce_scatter | solution.py:87
Sparse Core Ops, SparseCore 0:
  405.0 74.9 reduce-scatter.7
  484.2 88.2 reduce-scatter.3
  576.8 87.9 reduce-scatter.5
